TPU v7x, 32 devices: a whole 2x2x4 slice. The times are simulated.
32 devices in a mesh: dp: 8 (over z, x), mp: 4 (over y, core).
Axes of the slice: x: 2, y: 2, z: 4, core: 2. Of those that a mesh axis runs over, the one named last changes fastest.
Arguments:
- inputs: bfloat16 [2, 16384, 768], P(None, ('dp', 'mp')), may hold values from -6 to 6
- lengths: int32 [2, 32], P(None, 'dp'), may hold values from 64 to 512
- membership: int32 [2, 32, 8], replicated, may hold values from 0 to 1, as said below
- w_query: bfloat16 [768, 768], P(None, 'mp'), may hold values from -0.21875 to 0.21875
- b_query: bfloat16 [768], P('mp'), may hold values from -1.75 to 1.75
- w_key: bfloat16 [768, 768], P(None, 'mp'), may hold values from -0.21875 to 0.21875
- w_value: bfloat16 [768, 768], P(None, 'mp'), may hold values from -0.21875 to 0.21875
- b_value: bfloat16 [768], P('mp'), may hold values from -1.75 to 1.75
- w_output: bfloat16 [768, 768], P('mp'), may hold values from -0.875 to 0.875
- b_output: bfloat16 [768], replicated, may hold values from -0.625 to 0.625
- gain_first: bfloat16 [768], replicated, may hold values from 0.5 to 1.5
- bias_first: bfloat16 [768], replicated, may hold values from -0.625 to 0.625
- w_inner: bfloat16 [768, 3072], P(None, 'mp'), may hold values from -0.21875 to 0.21875
- b_inner: bfloat16 [3072], P('mp'), may hold values from -1.75 to 1.75
- w_outer: bfloat16 [3072, 768], P('mp'), may hold values from -0.109375 to 0.109375
- b_outer: bfloat16 [768], replicated, may hold values from -0.625 to 0.625
- gain_second: bfloat16 [768], replicated, may hold values from 0.5 to 1.5
- bias_second: bfloat16 [768], replicated, may hold values from -0.625 to 0.625
Outputs:
- outputs: bfloat16 [2, 16384, 768], P(None, ('dp', 'mp'))
- loss_total: float32 [], replicated
- grad_inputs: float32 [2, 16384, 768], P(None, ('dp', 'mp'))
- grad_w_query: float32 [768, 768], P(None, 'mp')
- grad_b_query: float32 [768], P('mp')
- grad_w_key: float32 [768, 768], P(None, 'mp')
- grad_w_value: float32 [768, 768], P(None, 'mp')
- grad_b_value: float32 [768], P('mp')
- grad_w_output: float32 [768, 768], P('mp')
- grad_b_output: float32 [768], replicated
- grad_gain_first: float32 [768], replicated
- grad_bias_first: float32 [768], replicated
- grad_w_inner: float32 [768, 3072], P(None, 'mp')
- grad_b_inner: float32 [3072], P('mp')
- grad_w_outer: float32 [3072, 768], P('mp')
- grad_b_outer: float32 [768], replicated
- grad_gain_second: float32 [768], replicated
- grad_bias_second: float32 [768], replicated
Inputs may be any that keep to these rules, and one draw needn't show every extreme that they name: `membership`: each row has a single 1. Each of the 8 groups holds 2 to 7 sentences, and some group holds exactly 7 in every draw.
All inputs are finite; a program needn't handle non-finite values.
Results may differ from a plain program's by a relative error of at most 0.015.
Values may be sent and summed in bfloat16 or wider, within the bound.
No kernel may reach another device: no remote copies, remote signals or barrier semaphores. Data moves between devices by JAX's collectives and lax.ppermute only.
A program may use at most 192 MiB of HBM per device.

v0:
```python
import math
import jax
import jax.numpy as jnp
from jax import lax
from jax.sharding import PartitionSpec as P

HEAD_DIM = 64
SEQ_LEN = 512
MICRO = 2
SENT_DEV = 1
eps_norm = 1e-05
eps_unit = 1e-06
cos_scale = 20.0


def layer_norm(row_values, norm_gain, norm_bias):
    centred = row_values - jnp.mean(row_values, axis=-1, keepdims=True)
    spread = jnp.mean(centred * centred, axis=-1, keepdims=True)
    return centred * lax.rsqrt(spread + eps_norm) * norm_gain + norm_bias


def gelu_exact(inner_pre):
    return jax.nn.gelu(inner_pre, approximate=False)


def attend_forward(packed):
    query_rows, key_heads, value_rows, length = packed
    inv_root = 1.0 / math.sqrt(query_rows.shape[-1])
    raw_scores = (
        jnp.einsum("qhd,khd->hqk", query_rows, key_heads, preferred_element_type=jnp.float32)
        * inv_root
    )
    allowed = jnp.arange(raw_scores.shape[-1]) < length
    masked = jnp.where(allowed[None, None, :], raw_scores, -1e30)
    row_top = jnp.max(masked, axis=-1, keepdims=True)
    raised = jnp.exp(masked - row_top)
    sum_all = jnp.sum(raised, axis=-1, keepdims=True)
    prob_low = (raised / sum_all).astype(jnp.bfloat16)
    context = jnp.einsum("hqk,khd->qhd", prob_low, value_rows, preferred_element_type=jnp.float32)
    return (context.astype(jnp.bfloat16), (row_top + jnp.log(sum_all))[:, :, 0])


def attend_backward(packed):
    query_rows, key_heads, value_rows, length, log_total, dcontext_rows = packed
    inv_root = 1.0 / math.sqrt(query_rows.shape[-1])
    raw_scores = (
        jnp.einsum("qhd,khd->hqk", query_rows, key_heads, preferred_element_type=jnp.float32)
        * inv_root
    )
    allowed = jnp.arange(raw_scores.shape[-1]) < length
    prob_rows = jnp.where(allowed[None, None, :], jnp.exp(raw_scores - log_total[:, :, None]), 0.0)
    dprobs = jnp.einsum(
        "qhd,khd->hqk", dcontext_rows, value_rows, preferred_element_type=jnp.float32
    )
    dvalues = jnp.einsum(
        "hqk,qhd->khd",
        prob_rows.astype(jnp.bfloat16),
        dcontext_rows,
        preferred_element_type=jnp.float32,
    )
    weighted = jnp.sum(prob_rows * dprobs, axis=-1, keepdims=True)
    dscores = (prob_rows * (dprobs - weighted)).astype(jnp.bfloat16)
    dqueries = (
        jnp.einsum("hqk,khd->qhd", dscores, key_heads, preferred_element_type=jnp.float32)
        * inv_root
    )
    dkey_heads = (
        jnp.einsum("hqk,qhd->khd", dscores, query_rows, preferred_element_type=jnp.float32)
        * inv_root
    )
    return (
        dqueries.astype(jnp.bfloat16),
        dkey_heads.astype(jnp.bfloat16),
        dvalues.astype(jnp.bfloat16),
    )


def shards(
    inputs,
    lengths,
    membership,
    w_query,
    b_query,
    w_key,
    w_value,
    b_value,
    w_output,
    b_output,
    gain_first,
    bias_first,
    w_inner,
    b_inner,
    w_outer,
    b_outer,
    gain_second,
    bias_second,
):
    groups = lax.axis_size("mp")
    model_rank = lax.axis_index("mp")
    local_width = w_query.shape[1]
    own_rows = inputs.shape[1]
    all_sents = membership.shape[1]
    own_start = (lax.axis_index("dp") * groups + model_rank) * SENT_DEV
    width = inputs.shape[2]
    full_query, full_bquery, full_key, full_value, full_bvalue, full_output = (
        w_query,
        b_query,
        w_key,
        w_value,
        b_value,
        w_output,
    )
    attn_width = full_query.shape[1]
    heads_attn = attn_width // HEAD_DIM
    w_joint = jnp.concatenate([full_query, full_key, full_value], axis=1)
    b_joint = jnp.concatenate([full_bquery, jnp.zeros_like(full_bquery), full_bvalue]).astype(
        jnp.float32
    )
    gain_one = gain_first.astype(jnp.float32)
    bias_one = bias_first.astype(jnp.float32)
    gain_two = gain_second.astype(jnp.float32)
    bias_two = bias_second.astype(jnp.float32)
    shift_output = b_output.astype(jnp.float32)
    shift_outer = b_outer.astype(jnp.float32)
    inner_weight, inner_bias, outer_weight = (w_inner, b_inner, w_outer)
    inner_shift = inner_bias.astype(jnp.float32)
    grad_joint = jnp.zeros(w_joint.shape, jnp.float32)
    grad_bjoint = jnp.zeros(b_joint.shape, jnp.float32)
    grad_wout = jnp.zeros(full_output.shape, jnp.float32)
    grad_inner = jnp.zeros(inner_weight.shape, jnp.float32)
    grad_binner = jnp.zeros(inner_bias.shape, jnp.float32)
    grad_outer = jnp.zeros(outer_weight.shape, jnp.float32)
    grad_boutput = jnp.zeros((width,), jnp.float32)
    grad_bouter = jnp.zeros((width,), jnp.float32)
    grad_gain_one = jnp.zeros((width,), jnp.float32)
    grad_bias_one = jnp.zeros((width,), jnp.float32)
    grad_gain_two = jnp.zeros((width,), jnp.float32)
    grad_bias_two = jnp.zeros((width,), jnp.float32)
    loss_local = jnp.zeros((), jnp.float32)
    outputs_list = []
    grad_list = []
    for micro_index in range(MICRO):
        own_inputs = inputs[micro_index]
        group_lengths = lengths[micro_index]
        own_lengths = lax.dynamic_slice_in_dim(group_lengths, model_rank * SENT_DEV, SENT_DEV)
        gathered = lax.all_gather(own_inputs, "mp", axis=0, tiled=True)
        attn_rows_count = gathered.shape[0]
        attn_sents = attn_rows_count // SEQ_LEN
        joint_rows = (
            jnp.dot(gathered, w_joint, preferred_element_type=jnp.float32) + b_joint
        ).astype(jnp.bfloat16)
        shaped = joint_rows.reshape(attn_sents, SEQ_LEN, 3, heads_attn, HEAD_DIM)
        queries = shaped[:, :, 0]
        key_heads = shaped[:, :, 1]
        values = shaped[:, :, 2]
        context, log_total = lax.map(attend_forward, (queries, key_heads, values, group_lengths))
        context = context.reshape(attn_rows_count, attn_width)
        attn_sum = lax.psum_scatter(
            jnp.dot(context, full_output, preferred_element_type=jnp.float32).astype(jnp.bfloat16),
            "mp",
            scatter_dimension=0,
            tiled=True,
        ).astype(jnp.float32)
        pre_first = attn_sum + shift_output + own_inputs.astype(jnp.float32)
        first_norm = layer_norm(pre_first, gain_one, bias_one)
        first_low = first_norm.astype(jnp.bfloat16)
        ffn_input = lax.all_gather(first_low, "mp", axis=0, tiled=True)
        inner_pre = (
            jnp.dot(ffn_input, inner_weight, preferred_element_type=jnp.float32) + inner_shift
        )
        hidden = gelu_exact(inner_pre).astype(jnp.bfloat16)
        ffn_sum = lax.psum_scatter(
            jnp.dot(hidden, outer_weight, preferred_element_type=jnp.float32).astype(jnp.bfloat16),
            "mp",
            scatter_dimension=0,
            tiled=True,
        ).astype(jnp.float32)
        pre_second = ffn_sum + shift_outer + first_norm
        second_norm = layer_norm(pre_second, gain_two, bias_two)
        outputs_list.append(second_norm.astype(jnp.bfloat16))
        valid_mask = (jnp.arange(SEQ_LEN)[None, :] < own_lengths[:, None]).astype(jnp.float32)
        counts = own_lengths.astype(jnp.float32)[:, None]
        pooled = (
            jnp.sum(second_norm.reshape(SENT_DEV, SEQ_LEN, width) * valid_mask[:, :, None], axis=1)
            / counts
        )
        rscale = lax.rsqrt(jnp.sum(pooled * pooled, axis=1, keepdims=True) + eps_unit)
        unit_rows = pooled * rscale
        every_unit = lax.all_gather(unit_rows, ("dp", "mp"), axis=0, tiled=True)
        groups_all = membership[micro_index].astype(jnp.float32)
        groups_own = lax.dynamic_slice_in_dim(groups_all, own_start, SENT_DEV, 0)
        itself = jnp.arange(all_sents)[None, :] == (own_start + jnp.arange(SENT_DEV))[:, None]
        positive = jnp.where(
            itself, 0.0, jnp.dot(groups_own, groups_all.T, preferred_element_type=jnp.float32)
        )
        logits = cos_scale * jnp.dot(
            unit_rows,
            every_unit.T,
            precision=lax.Precision.HIGHEST,
            preferred_element_type=jnp.float32,
        )
        others = jnp.where(itself, -1e30, logits)
        row_top = jnp.max(others, axis=1, keepdims=True)
        raised = jnp.exp(others - row_top)
        sum_all = jnp.sum(raised, axis=1, keepdims=True)
        sum_pos = jnp.sum(raised * positive, axis=1, keepdims=True)
        loss_local = loss_local + jnp.sum(jnp.log(sum_all) - jnp.log(sum_pos))
        dlogits = raised / sum_all - raised * positive / sum_pos
        dunits = cos_scale * jnp.dot(
            dlogits, every_unit, precision=lax.Precision.HIGHEST, preferred_element_type=jnp.float32
        )
        dkeys_all = cos_scale * jnp.dot(
            dlogits.T,
            unit_rows,
            precision=lax.Precision.HIGHEST,
            preferred_element_type=jnp.float32,
        )
        dunits = dunits + lax.psum_scatter(dkeys_all, ("dp", "mp"), scatter_dimension=0, tiled=True)
        dpooled = rscale * (dunits - unit_rows * jnp.sum(unit_rows * dunits, axis=1, keepdims=True))
        dsecond = ((valid_mask / counts)[:, :, None] * dpooled[:, None, :]).reshape(own_rows, width)
        dpre_second, dgain_two, dbias_two = jax.vjp(layer_norm, pre_second, gain_two, bias_two)[1](
            dsecond
        )
        grad_gain_two = grad_gain_two + dgain_two
        grad_bias_two = grad_bias_two + dbias_two
        grad_bouter = grad_bouter + jnp.sum(dpre_second, axis=0)
        dffn_low = dpre_second.astype(jnp.bfloat16)
        dffn_rows = lax.all_gather(dffn_low, "mp", axis=0, tiled=True)
        grad_outer = grad_outer + jnp.einsum(
            "tf,td->fd", hidden, dffn_rows, preferred_element_type=jnp.float32
        )
        dhidden = jnp.einsum(
            "td,fd->tf", dffn_rows, outer_weight, preferred_element_type=jnp.float32
        )
        dinner = jax.vjp(gelu_exact, inner_pre)[1](dhidden)[0].astype(jnp.bfloat16)
        grad_binner = grad_binner + jnp.sum(dinner, axis=0, dtype=jnp.float32)
        grad_inner = grad_inner + jnp.einsum(
            "td,tf->df", ffn_input, dinner, preferred_element_type=jnp.float32
        )
        dfirst_ffn = lax.psum_scatter(
            jnp.einsum(
                "tf,df->td", dinner, inner_weight, preferred_element_type=jnp.float32
            ).astype(jnp.bfloat16),
            "mp",
            scatter_dimension=0,
            tiled=True,
        ).astype(jnp.float32)
        dfirst = dfirst_ffn + dpre_second
        dpre_first, dgain_one, dbias_one = jax.vjp(layer_norm, pre_first, gain_one, bias_one)[1](
            dfirst
        )
        grad_gain_one = grad_gain_one + dgain_one
        grad_bias_one = grad_bias_one + dbias_one
        grad_boutput = grad_boutput + jnp.sum(dpre_first, axis=0)
        dattn_low = dpre_first.astype(jnp.bfloat16)
        dattn_all = lax.all_gather(dattn_low, "mp", axis=0, tiled=True)
        grad_wout = grad_wout + jnp.einsum(
            "tc,td->cd", context, dattn_all, preferred_element_type=jnp.float32
        )
        dcontext = jnp.einsum(
            "td,cd->tc", dattn_all, full_output, preferred_element_type=jnp.float32
        ).astype(jnp.bfloat16)
        dcontext_heads = dcontext.reshape(attn_sents, SEQ_LEN, heads_attn, HEAD_DIM)
        dqueries, dkey_heads, dvalues = lax.map(
            attend_backward, (queries, key_heads, values, group_lengths, log_total, dcontext_heads)
        )
        djoint = jnp.stack([dqueries, dkey_heads, dvalues], axis=2).reshape(
            attn_rows_count, 3 * attn_width
        )
        grad_bjoint = grad_bjoint + jnp.sum(djoint, axis=0, dtype=jnp.float32)
        grad_joint = grad_joint + jnp.einsum(
            "td,tc->dc", gathered, djoint, preferred_element_type=jnp.float32
        )
        grad_list.append(
            lax.psum_scatter(
                jnp.einsum("tc,dc->td", djoint, w_joint, preferred_element_type=jnp.float32).astype(
                    jnp.bfloat16
                ),
                "mp",
                scatter_dimension=0,
                tiled=True,
            ).astype(jnp.float32)
            + dpre_first
        )
    summed = lax.psum(
        (grad_joint, grad_bjoint, grad_wout, grad_inner, grad_binner, grad_outer), "dp"
    )
    small_sums = lax.psum(
        (
            grad_boutput,
            grad_gain_one,
            grad_bias_one,
            grad_bouter,
            grad_gain_two,
            grad_bias_two,
            loss_local,
        ),
        ("dp", "mp"),
    )
    joint_sum = summed[0]
    bias_sum = summed[1]
    return (
        jnp.stack(outputs_list),
        small_sums[6],
        jnp.stack(grad_list),
        joint_sum[:, :local_width],
        bias_sum[:local_width],
        joint_sum[:, local_width : 2 * local_width],
        joint_sum[:, 2 * local_width :],
        bias_sum[2 * local_width :],
        summed[2],
        small_sums[0],
        small_sums[1],
        small_sums[2],
        summed[3],
        summed[4],
        summed[5],
        small_sums[3],
        small_sums[4],
        small_sums[5],
    )


def solution(mesh):
    placed = (
        P(None, ("dp", "mp"), None),
        P(None, "dp"),
        P(),
        P(None, "mp"),
        P("mp"),
        P(None, "mp"),
        P(None, "mp"),
        P("mp"),
        P("mp", None),
        P(),
        P(),
        P(),
        P(None, "mp"),
        P("mp"),
        P("mp", None),
        P(),
        P(),
        P(),
    )
    return jax.shard_map(
        shards,
        mesh=mesh,
        in_specs=placed,
        out_specs=(
            P(None, ("dp", "mp"), None),
            P(),
            P(None, ("dp", "mp"), None),
            P(None, "mp"),
            P("mp"),
            P(None, "mp"),
            P(None, "mp"),
            P("mp"),
            P("mp", None),
            P(),
            P(),
            P(),
            P(None, "mp"),
            P("mp"),
            P("mp", None),
            P(),
            P(),
            P(),
        ),
        check_vma=False,
    )
```

profile of v0, /device:TPU:0, one launch (start us, length us, event | category | flops | bytes accessed | tf_op | source)
XLA Modules:
  0.0 1240.1 jit_solution(7503602419281284822)
XLA Ops:
  11.6 29.9 %all-gather.27.cloned.1.call-done = bf16[1,2048,768]{2,1,0:T(8,128)(2,1)} async-done(((bf16[1,512,768]{2,1,0:T(8,128)(2,1)}), bf16[1,2048,768]{2,1,0:T(8,128)(2,1)}) %all-gather.27.cloned.1.call-update) | async-done | bytes 3145744 | tf_op jit(solution)/shard_map/all_gather | solution.py:146
  41.5 5.3 fusion.132
  46.8 5.1 reshape.563
  54.9 19.9 %while.52 = (s32[]{:T(128)}, bf16[4,512,3,64]{1,3,2,0:T(8,128)(2,1)}, f32[4,3,512]{2,1,0:T(4,128)}, bf16[4,512,3,64]{1,3,2,0:T(8,128)(2,1)S(1)}, s32[4]{0:T(128)...) while((s32[]{:T(128)}, bf16[4,512,3,64]{1,3,2,0:T(8,128)(2,1)}, ...), condition=%wide.region_3.4_spmd, body=%wide.region_0.3_spmd.sunk | while | flops 210861056 | bytes 10283121 | solution.py:156
  77.4 5.9 fusion.135
  83.3 6.2 reshape.565
  96.7 21.2 %while.53 = (s32[]{:T(128)}, bf16[4,512,3,64]{1,3,2,0:T(8,128)(2,1)S(1)}, f32[4,3,512]{2,1,0:T(4,128)}, bf16[4,512,3,64]{1,3,2,0:T(8,128)(2,1)}, s32[4]{0:T(128)...) while((s32[]{:T(128)}, ...), condition=%wide.region_13.14_spmd, body=%wide.region_10.13_spmd.sunk | while | flops 210861056 | bytes 10283121 | solution.py:156
  123.7 10.4 reduce-scatter.9.cloned.1.call-done
  135.7 39.0 %reduce-scatter.13.cloned.1.call-done = bf16[512,768]{1,0:T(8,128)(2,1)} async-done(((bf16[2048,768]{1,0:T(8,128)(2,1)}), bf16[512,768]{1,0:T(8,128)(2,1)}) %reduce-scatter.13.cloned.1.call-update) | async-done | bytes 786448 | tf_op jit(solution)/shard_map/reduce_scatter | solution.py:158
  182.4 26.8 %all-gather.17.cloned.1.call-done = bf16[2048,768]{1,0:T(8,128)(2,1)} async-done(((bf16[512,768]{1,0:T(8,128)(2,1)}), bf16[2048,768]{1,0:T(8,128)(2,1)}) %all-gather.17.cloned.1.call-update) | async-done | bytes 3145744 | tf_op jit(solution)/shard_map/all_gather | solution.py:167
  209.2 7.2 fusion.212
  216.4 23.4 %all-gather.15.cloned.1.call-done = bf16[2048,768]{1,0:T(8,128)(2,1)} async-done(((bf16[512,768]{1,0:T(8,128)(2,1)}), bf16[2048,768]{1,0:T(8,128)(2,1)}) %all-gather.15.cloned.1.call-update) | async-done | bytes 3145744 | tf_op jit(solution)/shard_map/all_gather | solution.py:167
  239.8 33.0 %multiply_convert_fusion.3 = (bf16[2048,768]{1,0:T(8,128)(2,1)S(1)}, f32[2048,768]{1,0:T(8,128)}, bf16[2048,768]{1,0:T(8,128)(2,1)}, f32[2048,768]{1,0:T(8,128)}, f32[2048,768]{1,0:T(8,128)}) fusion(f32[768]{0:T(1024)} %convert_element_type.270, f32[2048,768]{1,0:T(8,128)} %fusion.212, bf16[2048,768]{1,0:T(8,128)(2,1)} %all-gather.15.cloned.1.call-done, ...), kind=kOutput, calls=%fused_computation.141 | convolution fusion | flops 2623537152 | bytes 35785728 | tf_op jit(solution)/shard_map/dot_general | solution.py:169
  274.5 3.9 convolution_convert_fusion.3
  278.5 6.6 convolution_convert_fusion.2
  300.0 16.6 %reduce-scatter.11.cloned.1.call-done = bf16[512,768]{1,0:T(8,128)(2,1)} async-done(((bf16[2048,768]{1,0:T(8,128)(2,1)}), bf16[512,768]{1,0:T(8,128)(2,1)}) %reduce-scatter.11.cloned.1.call-update) | async-done | bytes 786448 | tf_op jit(solution)/shard_map/reduce_scatter | solution.py:172
  316.6 40.7 %reduce-scatter.15.cloned.1.call-done = bf16[512,768]{1,0:T(8,128)(2,1)} async-done(((bf16[2048,768]{1,0:T(8,128)(2,1)}), bf16[512,768]{1,0:T(8,128)(2,1)}) %reduce-scatter.15.cloned.1.call-update) | async-done | bytes 786448 | tf_op jit(solution)/shard_map/reduce_scatter | solution.py:172
  372.8 40.8 %all-gather.4 = f32[32,1,768]{2,1,0:T(1,128)S(1)} all-gather(f32[1,1,768]{2,1,0:T(1,128)S(1)} %reshape.579), channel_id=4, replica_groups=mesh['dp'=8,'mp'=4] {'dp','mp'}, dimensions={0}, use_global_device_ids=true | all-gather | bytes 101376 | tf_op jit(solution)/shard_map/all_gather | solution.py:189
  413.5 37.1 %all-gather.5 = f32[32,1,768]{2,1,0:T(1,128)S(1)} all-gather(f32[1,1,768]{2,1,0:T(1,128)} %reshape.581), channel_id=5, replica_groups=mesh['dp'=8,'mp'=4] {'dp','mp'}, dimensions={0}, use_global_device_ids=true | all-gather | bytes 101376 | tf_op jit(solution)/shard_map/all_gather | solution.py:189
  468.6 119.6 %all-reduce.9.cloned.1.call-done = (f32[32,768]{1,0:T(8,128)}, f32[32,768]{1,0:T(8,128)}) async-done(((f32[32,768]{1,0:T(8,128)}, f32[32,768]{1,0:T(8,128)}), (f32[32,768]{1,0:T(8,128)}, f32[32,768]{1,0:T(8,128)})) %all-reduce.9.cloned.1.call-update) | async-done | bytes 196624
  594.0 3.9 fusion.145
  606.3 26.3 %all-gather.19.cloned.1.call-done = bf16[2048,768]{1,0:T(8,128)(2,1)} async-done(((bf16[512,768]{1,0:T(8,128)(2,1)}), bf16[2048,768]{1,0:T(8,128)(2,1)}) %all-gather.19.cloned.1.call-update) | async-done | bytes 3145744 | tf_op jit(solution)/shard_map/all_gather | solution.py:228
  632.7 7.6 fusion.213
  640.3 22.6 %all-gather.23.cloned.1.call-done = bf16[2048,768]{1,0:T(8,128)(2,1)} async-done(((bf16[512,768]{1,0:T(8,128)(2,1)}), bf16[2048,768]{1,0:T(8,128)(2,1)}) %all-gather.23.cloned.1.call-update) | async-done | bytes 3145744 | tf_op jit(solution)/shard_map/all_gather | solution.py:228
  662.8 16.7 %convert_reduce_fusion = (f32[768]{0:T(1024)}, bf16[2048,768]{1,0:T(8,128)(2,1)}, f32[768]{0:T(1024)}, bf16[2048,768]{1,0:T(8,128)(2,1)S(1)}) fusion(f32[2048,768]{1,0:T(8,128)} %get-tuple-element.443, f32[2048,768]{1,0:T(8,128)} %fusion.212, f32[768]{0:T(1024)S(1)} %copy-done.87, f32[2048,768]{1,0:T(8,128)} %fusion.213, ...), kind=kOutput, calls=%fused_computation.124 | convolution fusion | flops 2469394944 | bytes 42083328 | tf_op jit(solution)/shard_map/td,fd->tf/dot_general | solution.py:232
  681.1 4.0 convolution_convert_fusion.1
  685.2 6.2 convolution_convert_fusion
  691.6 31.7 %reduce-scatter.17.cloned.1.call-done = bf16[512,768]{1,0:T(8,128)(2,1)} async-done(((bf16[2048,768]{1,0:T(8,128)(2,1)}), bf16[512,768]{1,0:T(8,128)(2,1)}) %reduce-scatter.17.cloned.1.call-update) | async-done | bytes 786448 | tf_op jit(solution)/shard_map/reduce_scatter | solution.py:240
  723.3 40.7 %reduce-scatter.21.cloned.1.call-done = bf16[512,768]{1,0:T(8,128)(2,1)} async-done(((bf16[2048,768]{1,0:T(8,128)(2,1)}), bf16[512,768]{1,0:T(8,128)(2,1)}) %reduce-scatter.21.cloned.1.call-update) | async-done | bytes 786448 | tf_op jit(solution)/shard_map/reduce_scatter | solution.py:240
  764.0 5.1 multiply_reduce_fusion.5
  770.5 4.1 fusion.192
  778.6 27.0 %all-gather.21.cloned.1.call-done = bf16[2048,768]{1,0:T(8,128)(2,1)} async-done(((bf16[512,768]{1,0:T(8,128)(2,1)}), bf16[2048,768]{1,0:T(8,128)(2,1)}) %all-gather.21.cloned.1.call-update) | async-done | bytes 3145744 | tf_op jit(solution)/shard_map/all_gather | solution.py:256
  805.6 3.9 convolution_convert_fusion.9
  812.1 24.0 %all-gather.25.cloned.1.call-done = bf16[2048,768]{1,0:T(8,128)(2,1)} async-done(((bf16[512,768]{1,0:T(8,128)(2,1)}), bf16[2048,768]{1,0:T(8,128)(2,1)}) %all-gather.25.cloned.1.call-update) | async-done | bytes 3145744 | tf_op jit(solution)/shard_map/all_gather | solution.py:256
  836.1 3.9 convolution_convert_fusion.8
  840.1 3.1 reshape.571
  848.2 40.0 %while.55 = (s32[]{:T(128)}, bf16[4,512,3,64]{1,3,2,0:T(8,128)(2,1)}, bf16[4,512,3,64]{1,3,2,0:T(8,128)(2,1)}, bf16[4,512,3,64]{1,3,2,0:T(8,128)(2,1)}, bf16[4,5...) while((s32[]{:T(128)}, ...), condition=%wide.region_51.52_spmd, body=%wide.region_49.51_spmd.sunk | while | flops 510884864 | bytes 25598088 | solution.py:264
  894.3 4.0 convolution_convert_fusion.4
  901.3 36.2 %while.54 = (s32[]{:T(128)}, bf16[4,512,3,64]{1,3,2,0:T(8,128)(2,1)}, bf16[4,512,3,64]{1,3,2,0:T(8,128)(2,1)}, bf16[4,512,3,64]{1,3,2,0:T(8,128)(2,1)}, bf16[4,5...) while((s32[]{:T(128)}, ...), condition=%wide.region_40.41_spmd, body=%wide.region_38.40_spmd.sunk | while | flops 510884864 | bytes 25598088 | solution.py:264
  942.5 4.0 convolution_convert_fusion.5
  947.1 5.7 fusion.216
  956.5 4.2 convolution_add_fusion
  960.7 4.2 convolution_add_fusion.1
  971.2 3.2 add_bitcast_fusion
  984.1 22.7 %all-reduce.4 = (f32[576]{0:T(1024)S(1)}, f32[768]{0:T(1024)}) all-reduce(f32[576]{0:T(1024)S(1)} %add.355, f32[768]{0:T(1024)S(1)} %add.361), channel_id=1, replica_groups=mesh['dp'=8,'mp'=4] {'dp'}, use_global_device_ids=true, to_apply=%region_56.57 | all-reduce | flops 1344 | bytes 10752 | tf_op jit(solution)/shard_map/psum | solution.py:285
  1013.0 41.8 %all-reduce.2 = (f32[]{:T(128)}, f32[768]{0:T(1024)}, f32[768]{0:T(1024)}, f32[768]{0:T(1024)}, f32[768]{0:T(1024)}, /*index=5*/f32[768]{0:T(1024)}, f32[768]{0:T(1024)}) all-reduce(f32[]{:T(128)S(6)} %add.345, f32[768]{0:T(1024)S(1)} %add.357, f32[768]{0:T(1024)S(1)} %add.358, ...), channel_id=1, replica_groups=mesh['dp'=8,'mp'=4] {'dp','mp'}, use_global_device_ids=true, to_apply=%region_30.31 | all-reduce | flops 4609 | bytes 36872 | tf_op jit(solution)/shard_map/psum | solution.py:288
  1054.8 3.8 pad_maximum_fusion
  1058.6 167.9 %all-reduce.11.cloned.1.call-done = (f32[768,576]{0,1:T(8,128)}, f32[192,768]{1,0:T(8,128)}, f32[768,768]{1,0:T(8,128)}, f32[768,768]{1,0:T(8,128)}) async-done(((f32[768,576]{0,1:T(8,128)}, f32[192,768]{1,0:T(8,128)}, f32[768,768]{1,0:T(8,128)}, f32[768,768]{1,0:T(8,128)}), (f32[768,576]{0,1:T(8,128)}, f32[192,768]{1,0:T(8,128)}, f32[768,768]{1,0:T(8,128)}, ...) | async-done | bytes 7077904 | tf_op jit(solution)/shard_map/psum | solution.py:285
  (500 shorter events, 268.0 us)
Async XLA Ops:
  7.2 202.0 %copy-start = (bf16[768,768]{1,0:T(8,128)(2,1)S(1)}, bf16[768,768]{1,0:T(8,128)(2,1)}, u32[]{:S(2)}) copy-start(bf16[768,768]{1,0:T(8,128)(2,1)} %param.38) | copy-start | bytes 3538948
  7.3 34.2 %all-gather.27.cloned.1.call-start = ((), (), s32[]{:S(2)}) async-start(), calls=%async_computation.22 | async-start | bytes 3932160 | tf_op jit(solution)/shard_map/all_gather | solution.py:146
  10.1 67.4 %all-gather.29.cloned.1.call-start = ((), (), s32[]{:S(2)}) async-start(), calls=%async_computation.23 | async-start | bytes 3932160 | tf_op jit(solution)/shard_map/all_gather | solution.py:146
  10.8 123.3 %reduce-scatter.9.cloned.1.call-start = ((), (), s32[]{:S(2)}) async-start(), calls=%async_computation.8 | async-start | bytes 3932160 | tf_op jit(solution)/shard_map/reduce_scatter | solution.py:158
  11.5 30.0 %copy-start.49 = (bf16[768,576]{0,1:T(8,128)(2,1)}, bf16[768,576]{0,1:T(8,128)(2,1)S(1)}, u32[]{:S(2)}) copy-start(bf16[768,576]{0,1:T(8,128)(2,1)S(1)} %constant_dynamic-update-slice_fusion) | copy-start | bytes 2654212
  74.9 8.4 copy-start.12
  74.9 8.4 copy-start.14
  74.9 8.4 copy-start.92
  77.4 15.9 %copy-start.25 = (bf16[24,8,4,512]{3,1,2,0:T(8,128)(2,1)}, bf16[24,8,4,512]{3,1,2,0:T(8,128)(2,1)S(1)}, u32[]{:S(2)}) copy-start(bf16[24,8,4,512]{3,1,2,0:T(8,128)(2,1)S(1)} %copy.108) | copy-start | bytes 2359300
  96.0 78.6 %reduce-scatter.13.cloned.1.call-start = ((), (), s32[]{:S(2)}) async-start(), calls=%async_computation.11 | async-start | bytes 3932160 | tf_op jit(solution)/shard_map/reduce_scatter | solution.py:158
  122.4 11.7 copy-start.1
  122.4 86.8 %all-gather.17.cloned.1.call-start = ((), (), s32[]{:S(2)}) async-start(), calls=%async_computation.12 | async-start | bytes 3932160 | tf_op jit(solution)/shard_map/all_gather | solution.py:167
  134.1 44.3 %copy-start.6 = (bf16[512,768]{1,0:T(8,128)(2,1)S(1)}, bf16[512,768]{1,0:T(8,128)(2,1)}, u32[]{:S(2)}) copy-start(bf16[512,768]{1,0:T(8,128)(2,1)} %reduce-scatter.9.cloned.1.call-done) | copy-start | bytes 2359300
  135.7 221.6 %copy-start.54 = (f32[512]{0:T(512)}, f32[512]{0:T(512)S(1)}, u32[]{:S(2)}) copy-start(f32[512]{0:T(512)S(1)} %broadcast_multiply_fusion.7) | copy-start | bytes 6148
  176.8 180.5 %copy-start.52 = (f32[512]{0:T(512)}, f32[512]{0:T(512)S(1)}, u32[]{:S(2)}) copy-start(f32[512]{0:T(512)S(1)} %broadcast_multiply_fusion.5) | copy-start | bytes 6148
  180.5 59.3 %all-gather.15.cloned.1.call-start = ((), (), s32[]{:S(2)}) async-start(), calls=%async_computation.9 | async-start | bytes 3932160 | tf_op jit(solution)/shard_map/all_gather | solution.py:167
  181.1 135.5 %reduce-scatter.11.cloned.1.call-start = ((), (), s32[]{:S(2)}) async-start(), calls=%async_computation.10 | async-start | bytes 3932160 | tf_op jit(solution)/shard_map/reduce_scatter | solution.py:172
  239.8 34.7 %copy-start.101 = (bf16[768,768]{1,0:T(8,128)(2,1)S(1)}, bf16[768,768]{1,0:T(8,128)(2,1)}, u32[]{:S(2)}) copy-start(bf16[768,768]{1,0:T(8,128)(2,1)} %param.40) | copy-start | bytes 3538948
  278.5 78.8 %reduce-scatter.15.cloned.1.call-start = ((), (), s32[]{:S(2)}) async-start(), calls=%async_computation.13 | async-start | bytes 3932160 | tf_op jit(solution)/shard_map/reduce_scatter | solution.py:172
  285.2 303.1 %all-reduce.9.cloned.1.call-start = ((), (), s32[]{:S(2)}) async-start(), calls=%async_computation.24 | async-start | bytes 393216
  467.3 165.4 %all-gather.19.cloned.1.call-start = ((), (), s32[]{:S(2)}) async-start(), calls=%async_computation.14 | async-start | bytes 3932160 | tf_op jit(solution)/shard_map/all_gather | solution.py:228
  588.2 9.7 copy-start.78
  588.2 9.7 copy-start.76
  588.2 9.7 copy-start.3
  588.2 9.8 copy-start.5
  588.3 9.8 copy-start.57
  588.3 9.8 copy-start.59
  588.3 9.8 copy-start.61
  588.3 9.8 copy-start.67
  588.3 9.8 copy-start.69
  588.3 9.8 copy-start.72
  588.3 9.8 copy-start.73
  603.1 59.8 %all-gather.23.cloned.1.call-start = ((), (), s32[]{:S(2)}) async-start(), calls=%async_computation.18 | async-start | bytes 3932160 | tf_op jit(solution)/shard_map/all_gather | solution.py:228
  603.8 36.5 %copy-start.71 = (f32[512]{0:T(512)}, f32[512]{0:T(512)S(1)}, u32[]{:S(2)}) copy-start(f32[512]{0:T(512)S(1)} %negate_multiply_fusion.3) | copy-start | bytes 6148
  606.3 117.0 %reduce-scatter.17.cloned.1.call-start = ((), (), s32[]{:S(2)}) async-start(), calls=%async_computation.15 | async-start | bytes 3932160 | tf_op jit(solution)/shard_map/reduce_scatter | solution.py:240
  606.3 56.5 %copy-start.87 = (f32[768]{0:T(1024)S(1)}, f32[768]{0:T(1024)}, u32[]{:S(2)}) copy-start(f32[768]{0:T(1024)} %convert_element_type.270) | copy-start | bytes 9220
  685.2 78.8 %reduce-scatter.21.cloned.1.call-start = ((), (), s32[]{:S(2)}) async-start(), calls=%async_computation.19 | async-start | bytes 3932160 | tf_op jit(solution)/shard_map/reduce_scatter | solution.py:240
  691.5 72.5 %copy-start.53 = (f32[512]{0:T(512)S(1)}, f32[512]{0:T(512)}, u32[]{:S(2)}) copy-start(f32[512]{0:T(512)} %copy-done.52) | copy-start | bytes 6148
  691.5 72.5 %copy-start.55 = (f32[512]{0:T(512)S(1)}, f32[512]{0:T(512)}, u32[]{:S(2)}) copy-start(f32[512]{0:T(512)} %copy-done.54) | copy-start | bytes 6148
  691.5 114.0 %all-gather.21.cloned.1.call-start = ((), (), s32[]{:S(2)}) async-start(), calls=%async_computation.16 | async-start | bytes 3932160 | tf_op jit(solution)/shard_map/all_gather | solution.py:256
  775.8 29.8 %copy-start.43 = (bf16[192,768]{1,0:T(8,128)(2,1)S(1)}, bf16[192,768]{1,0:T(8,128)(2,1)}, u32[]{:S(2)}) copy-start(bf16[192,768]{1,0:T(8,128)(2,1)} %param.34) | copy-start | bytes 884740
  776.9 59.3 %all-gather.25.cloned.1.call-start = ((), (), s32[]{:S(2)}) async-start(), calls=%async_computation.20 | async-start | bytes 3932160 | tf_op jit(solution)/shard_map/all_gather | solution.py:256
  778.5 228.3 %reduce-scatter.23.cloned.1.call-start = ((), (), s32[]{:S(2)}) async-start(), calls=%async_computation.21 | async-start | bytes 3932160 | tf_op jit(solution)/shard_map/reduce_scatter | solution.py:275
  809.5 26.6 %copy-start.44 = (bf16[192,768]{1,0:T(8,128)(2,1)S(1)}, bf16[192,768]{1,0:T(8,128)(2,1)}, u32[]{:S(2)}) copy-start(bf16[192,768]{1,0:T(8,128)(2,1)} %param.34) | copy-start | bytes 884740
  898.3 111.6 %reduce-scatter.19.cloned.1.call-start = ((), (), s32[]{:S(2)}) async-start(), calls=%async_computation.17 | async-start | bytes 3932160 | tf_op jit(solution)/shard_map/reduce_scatter | solution.py:275
  946.6 280.0 %all-reduce.11.cloned.1.call-start = ((), (), s32[]{:S(2)}) async-start(), calls=%async_computation.25 | async-start | bytes 14155776 | tf_op jit(solution)/shard_map/psum | solution.py:285
  977.3 32.6 %copy-start.21 = (f32[512,768]{1,0:T(8,128)S(1)}, f32[512,768]{1,0:T(8,128)}, u32[]{:S(2)}) copy-start(f32[512,768]{1,0:T(8,128)} %copy-done.20) | copy-start | bytes 4718596
  979.8 30.1 %copy-start.80 = (f32[512]{0:T(512)S(1)}, f32[512]{0:T(512)}, u32[]{:S(2)}) copy-start(f32[512]{0:T(512)} %copy-done.79) | copy-start | bytes 6148
  (75 other events, 222.3 us)
Sparse Core Ops, SparseCore 0:
  10.2 31.2 all-gather.26
  43.6 28.5 all-gather.28
  96.1 37.9 reduce-scatter.8
  136.7 37.9 reduce-scatter.12
  180.6 28.5 all-gather.16
  211.2 28.5 all-gather.14
  278.6 37.9 reduce-scatter.10
  319.3 37.9 reduce-scatter.14
  467.4 120.8 all-reduce.8
  603.2 29.4 all-gather.18
  634.2 28.5 all-gather.22
  685.3 37.9 reduce-scatter.16
  726.0 37.9 reduce-scatter.20
  777.0 28.5 all-gather.20
  807.5 28.5 all-gather.24
  898.5 37.9 reduce-scatter.22
  946.7 37.9 reduce-scatter.18
  989.6 236.9 all-reduce.10
where the time goes:
time: 1250 us; the launch traced here: 1240 us
  waiting for transfers between devices  648 us (52%)
  matrix products  225 us (18%)
  blocking collectives  142 us (11%)
  other arithmetic  119 us (10%)
  local copies, waits for them, and re-layouts  83.1 us (7%)
  between operations  21.2 us (2%)
    psum x1, waiting for transfers between devices, shards(): lax.psum((grad_joint, grad_bjoint, grad_wout, grad_inner, grad_binner, gr...  168 us
    unnamed x19, waiting for transfers between devices  121 us
    all_gather x2, blocking collectives, shards(): every_unit = lax.all_gather(unit_rows, ('dp', 'mp'), axis=0, tiled=True)  77.9 us
    reduce_scatter x2, waiting for transfers between devices, shards(): lax.psum_scatter(jnp.einsum('tf,df->td', dinner, inner_weight, preferred_...  72.4 us
    reduce_scatter x2, waiting for transfers between devices, shards(): lax.psum_scatter(jnp.dot(hidden, outer_weight, preferred_element_type=jnp...  57.3 us
    all_gather x2, waiting for transfers between devices, shards(): dattn_all = lax.all_gather(dattn_low, 'mp', axis=0, tiled=True)  51 us
    all_gather x2, waiting for transfers between devices, shards(): ffn_input = lax.all_gather(first_low, 'mp', axis=0, tiled=True)  50.2 us
    reduce_scatter x2, waiting for transfers between devices, shards(): lax.psum_scatter(jnp.dot(context, full_output, preferred_element_type=jnp...  49.4 us
  transfers between devices with their start and end apart: 18, of which 15 were waited for; matrix products, arithmetic and copies ran while one was open for 17% of the time, Pallas kernels for 0%

commit v1 on v0

--- a/solution.py
+++ b/solution.py
@@ -11,6 +11,19 @@
 eps_norm = 1e-05
 eps_unit = 1e-06
 cos_scale = 20.0
+
+
+def collect(shard, axis, dim):
+    ways = lax.axis_size(axis)
+    up = [(d, (d + 1) % ways) for d in range(ways)]
+    down = [(d, (d - 1) % ways) for d in range(ways)]
+    earlier, later = ([shard], [shard])
+    for _ in range(ways // 2):
+        earlier.append(lax.ppermute(earlier[-1], axis, up))
+    for _ in range((ways - 1) // 2):
+        later.append(lax.ppermute(later[-1], axis, down))
+    line = jnp.concatenate([*earlier[::-1], *later[1:]], axis=dim)
+    return jnp.roll(line, (lax.axis_index(axis) - ways // 2) * shard.shape[dim], axis=dim)
 
 
 def layer_norm(row_values, norm_gain, norm_bias):
@@ -143,7 +156,7 @@
         own_inputs = inputs[micro_index]
         group_lengths = lengths[micro_index]
         own_lengths = lax.dynamic_slice_in_dim(group_lengths, model_rank * SENT_DEV, SENT_DEV)
-        gathered = lax.all_gather(own_inputs, "mp", axis=0, tiled=True)
+        gathered = collect(own_inputs, "mp", 0)
         attn_rows_count = gathered.shape[0]
         attn_sents = attn_rows_count // SEQ_LEN
         joint_rows = (

time: 1250 us -> 1300 us (1.040)
  other arithmetic: 119 us -> 154 us
    concatenate x0 -> x2, other arithmetic: none -> 35.6 us  [collect(): jnp.roll(line, (lax.axis_index(axis) - ways // 2) * shard.shape[dim], axi...]
    ppermute x0 -> x6, waiting for transfers between devices: none -> 32.9 us  [the longest x4 32.9 us: collect(): earlier.append(lax.ppermute(earlier[-1], axis, up))]
    all_gather x2 -> x0, waiting for transfers between devices: 29.9 us -> none  [shards(): gathered = lax.all_gather(own_inputs, 'mp', axis=0, tiled=True)]
    unnamed x19 -> x17, waiting for transfers between devices: 121 us -> 120 us
  transfers between devices with their start and end apart: 18 -> 22, of which waited for: 15 -> 17; matrix products, arithmetic and copies ran while one was open for 17% -> 18% of each run, Pallas kernels for 0% -> 0%
where the time goes in v1:
time: 1300 us; the launch traced here: 1290 us
  waiting for transfers between devices  653 us (50%)
  matrix products  221 us (17%)
  other arithmetic  154 us (12%)
  blocking collectives  142 us (11%)
  local copies, waits for them, and re-layouts  89.7 us (7%)
  between operations  20.9 us (2%)
    psum x1, waiting for transfers between devices, shards(): lax.psum((grad_joint, grad_bjoint, grad_wout, grad_inner, grad_binner, gr...  168 us
    unnamed x17, waiting for transfers between devices  120 us
    all_gather x2, blocking collectives, shards(): every_unit = lax.all_gather(unit_rows, ('dp', 'mp'), axis=0, tiled=True)  77.9 us
    reduce_scatter x2, waiting for transfers between devices, shards(): lax.psum_scatter(jnp.einsum('tf,df->td', dinner, inner_weight, preferred_...  72.4 us
    reduce_scatter x2, waiting for transfers between devices, shards(): lax.psum_scatter(jnp.dot(hidden, outer_weight, preferred_element_type=jnp...  57.2 us
    reduce_scatter x2, waiting for transfers between devices, shards(): lax.psum_scatter(jnp.dot(context, full_output, preferred_element_type=jnp...  51.7 us
    all_gather x2, waiting for transfers between devices, shards(): dattn_all = lax.all_gather(dattn_low, 'mp', axis=0, tiled=True)  51.1 us
    all_gather x2, waiting for transfers between devices, shards(): ffn_input = lax.all_gather(first_low, 'mp', axis=0, tiled=True)  50.2 us
  transfers between devices with their start and end apart: 22, of which 17 were waited for; matrix products, arithmetic and copies ran while one was open for 18% of the time, Pallas kernels for 0%

profile of v1, /device:TPU:0, one launch (start us, length us, event | category | flops | bytes accessed | tf_op | source)
XLA Modules:
  0.0 1291.2 jit_solution(2133789577934941849)
XLA Ops:
  12.8 14.7 %collective-permute-done = bf16[512,768]{1,0:T(8,128)(2,1)S(1)} collective-permute-done((bf16[512,768]{1,0:T(8,128)(2,1)S(1)}, bf16[512,768]{1,0:T(8,128)(2,1)S(1)}, u32[]{:S(2)}, u32[]{:S(2)}) %collective-permute-start) | collective-permute-done | bytes 786464 | tf_op jit(solution)/shard_map/ppermute | solution.py:22
  33.1 8.8 collective-permute-done.3
  42.0 4.3 collective-permute-start.4
  46.3 9.3 collective-permute-done.1
  55.6 25.7 %fusion.130 = bf16[2048,768]{1,0:T(8,128)(2,1)S(1)} fusion(s32[]{:T(128)S(6)} %select_n.57, bf16[512,768]{1,0:T(8,128)(2,1)} %collective-permute-done.1, bf16[512,768]{1,0:T(8,128)(2,1)S(1)} %collective-permute-done, bf16[512,768]{1,0:T(8,128)(2,1)S(1)} %get-tuple-element.431, bf16[512,768]{1,0:T(8,128)(2,1)S(1)} %collective-permute-done.2), kind=kLoop, calls=%fused_computation.194 | loop fusion | flops 25165824 | bytes 6291460 | tf_op jit(solution)/shard_map/jit(_roll_dynamic)/concatenate | solution.py:26
  86.4 5.3 reshape.563
  94.6 19.9 %while.52 = (s32[]{:T(128)}, bf16[4,512,3,64]{1,3,2,0:T(8,128)(2,1)}, f32[4,3,512]{2,1,0:T(4,128)}, bf16[4,512,3,64]{1,3,2,0:T(8,128)(2,1)S(1)}, s32[4]{0:T(128)...) while((s32[]{:T(128)}, bf16[4,512,3,64]{1,3,2,0:T(8,128)(2,1)}, ...), condition=%wide.region_3.5_spmd, body=%wide.region_0.4_spmd.sunk | while | flops 210861056 | bytes 10283121 | solution.py:169
  117.1 9.9 fusion.123
  132.3 6.4 reshape.565
  145.9 21.1 %while.53 = (s32[]{:T(128)}, bf16[4,512,3,64]{1,3,2,0:T(8,128)(2,1)S(1)}, f32[4,3,512]{2,1,0:T(4,128)}, bf16[4,512,3,64]{1,3,2,0:T(8,128)(2,1)}, s32[4]{0:T(128)...) while((s32[]{:T(128)}, ...), condition=%wide.region_13.15_spmd, body=%wide.region_10.14_spmd.sunk | while | flops 210861056 | bytes 10283121 | solution.py:169
  172.7 12.6 reduce-scatter.9.cloned.1.call-done
  186.9 39.1 %reduce-scatter.13.cloned.1.call-done = bf16[512,768]{1,0:T(8,128)(2,1)} async-done(((bf16[2048,768]{1,0:T(8,128)(2,1)}), bf16[512,768]{1,0:T(8,128)(2,1)}) %reduce-scatter.13.cloned.1.call-update) | async-done | bytes 786448 | tf_op jit(solution)/shard_map/reduce_scatter | solution.py:171
  233.8 26.8 %all-gather.13.cloned.1.call-done = bf16[2048,768]{1,0:T(8,128)(2,1)} async-done(((bf16[512,768]{1,0:T(8,128)(2,1)}), bf16[2048,768]{1,0:T(8,128)(2,1)}) %all-gather.13.cloned.1.call-update) | async-done | bytes 3145744 | tf_op jit(solution)/shard_map/all_gather | solution.py:180
  260.6 7.2 fusion.207
  267.7 23.4 %all-gather.11.cloned.1.call-done = bf16[2048,768]{1,0:T(8,128)(2,1)} async-done(((bf16[512,768]{1,0:T(8,128)(2,1)}), bf16[2048,768]{1,0:T(8,128)(2,1)}) %all-gather.11.cloned.1.call-update) | async-done | bytes 3145744 | tf_op jit(solution)/shard_map/all_gather | solution.py:180
  291.1 33.1 %multiply_convert_fusion.3 = (bf16[2048,768]{1,0:T(8,128)(2,1)S(1)}, f32[2048,768]{1,0:T(8,128)}, bf16[2048,768]{1,0:T(8,128)(2,1)}, f32[2048,768]{1,0:T(8,128)}, f32[2048,768]{1,0:T(8,128)}) fusion(f32[768]{0:T(1024)} %convert_element_type.263, f32[2048,768]{1,0:T(8,128)} %fusion.207, bf16[2048,768]{1,0:T(8,128)(2,1)} %all-gather.11.cloned.1.call-done, ...), kind=kOutput, calls=%fused_computation.157 | convolution fusion | flops 2623537152 | bytes 35785728 | tf_op jit(solution)/shard_map/dot_general | solution.py:182
  326.0 3.9 convolution_convert_fusion.3
  330.0 6.6 convolution_convert_fusion.2
  351.4 16.6 %reduce-scatter.11.cloned.1.call-done = bf16[512,768]{1,0:T(8,128)(2,1)} async-done(((bf16[2048,768]{1,0:T(8,128)(2,1)}), bf16[512,768]{1,0:T(8,128)(2,1)}) %reduce-scatter.11.cloned.1.call-update) | async-done | bytes 786448 | tf_op jit(solution)/shard_map/reduce_scatter | solution.py:185
  368.1 40.5 %reduce-scatter.15.cloned.1.call-done = bf16[512,768]{1,0:T(8,128)(2,1)} async-done(((bf16[2048,768]{1,0:T(8,128)(2,1)}), bf16[512,768]{1,0:T(8,128)(2,1)}) %reduce-scatter.15.cloned.1.call-update) | async-done | bytes 786448 | tf_op jit(solution)/shard_map/reduce_scatter | solution.py:185
  424.1 40.8 %all-gather.2 = f32[32,1,768]{2,1,0:T(1,128)S(1)} all-gather(f32[1,1,768]{2,1,0:T(1,128)S(1)} %reshape.575), channel_id=2, replica_groups=mesh['dp'=8,'mp'=4] {'dp','mp'}, dimensions={0}, use_global_device_ids=true | all-gather | bytes 101376 | tf_op jit(solution)/shard_map/all_gather | solution.py:202
  464.9 37.1 %all-gather.3 = f32[32,1,768]{2,1,0:T(1,128)S(1)} all-gather(f32[1,1,768]{2,1,0:T(1,128)} %reshape.577), channel_id=3, replica_groups=mesh['dp'=8,'mp'=4] {'dp','mp'}, dimensions={0}, use_global_device_ids=true | all-gather | bytes 101376 | tf_op jit(solution)/shard_map/all_gather | solution.py:202
  519.9 119.6 %all-reduce.9.cloned.1.call-done = (f32[32,768]{1,0:T(8,128)}, f32[32,768]{1,0:T(8,128)}) async-done(((f32[32,768]{1,0:T(8,128)}, f32[32,768]{1,0:T(8,128)}), (f32[32,768]{1,0:T(8,128)}, f32[32,768]{1,0:T(8,128)})) %all-reduce.9.cloned.1.call-update) | async-done | bytes 196624
  657.4 26.3 %all-gather.15.cloned.1.call-done = bf16[2048,768]{1,0:T(8,128)(2,1)} async-done(((bf16[512,768]{1,0:T(8,128)(2,1)}), bf16[2048,768]{1,0:T(8,128)(2,1)}) %all-gather.15.cloned.1.call-update) | async-done | bytes 3145744 | tf_op jit(solution)/shard_map/all_gather | solution.py:241
  683.7 7.6 fusion.208
  691.3 22.6 %all-gather.19.cloned.1.call-done = bf16[2048,768]{1,0:T(8,128)(2,1)} async-done(((bf16[512,768]{1,0:T(8,128)(2,1)}), bf16[2048,768]{1,0:T(8,128)(2,1)}) %all-gather.19.cloned.1.call-update) | async-done | bytes 3145744 | tf_op jit(solution)/shard_map/all_gather | solution.py:241
  713.9 16.7 %convert_reduce_fusion = (f32[768]{0:T(1024)}, bf16[2048,768]{1,0:T(8,128)(2,1)}, f32[768]{0:T(1024)}, bf16[2048,768]{1,0:T(8,128)(2,1)S(1)}) fusion(f32[2048,768]{1,0:T(8,128)} %get-tuple-element.444, f32[2048,768]{1,0:T(8,128)} %fusion.207, f32[768]{0:T(1024)S(1)} %copy-done.89, f32[2048,768]{1,0:T(8,128)} %fusion.208, ...), kind=kOutput, calls=%fused_computation.140 | convolution fusion | flops 2469394944 | bytes 42083328 | tf_op jit(solution)/shard_map/td,fd->tf/dot_general | solution.py:245
  732.2 4.0 convolution_convert_fusion.1
  736.3 6.2 convolution_convert_fusion
  742.6 31.7 %reduce-scatter.17.cloned.1.call-done = bf16[512,768]{1,0:T(8,128)(2,1)} async-done(((bf16[2048,768]{1,0:T(8,128)(2,1)}), bf16[512,768]{1,0:T(8,128)(2,1)}) %reduce-scatter.17.cloned.1.call-update) | async-done | bytes 786448 | tf_op jit(solution)/shard_map/reduce_scatter | solution.py:253
  774.3 40.7 %reduce-scatter.21.cloned.1.call-done = bf16[512,768]{1,0:T(8,128)(2,1)} async-done(((bf16[2048,768]{1,0:T(8,128)(2,1)}), bf16[512,768]{1,0:T(8,128)(2,1)}) %reduce-scatter.21.cloned.1.call-update) | async-done | bytes 786448 | tf_op jit(solution)/shard_map/reduce_scatter | solution.py:253
  815.0 5.0 multiply_reduce_fusion.5
  821.5 4.1 fusion.188
  829.6 27.0 %all-gather.17.cloned.1.call-done = bf16[2048,768]{1,0:T(8,128)(2,1)} async-done(((bf16[512,768]{1,0:T(8,128)(2,1)}), bf16[2048,768]{1,0:T(8,128)(2,1)}) %all-gather.17.cloned.1.call-update) | async-done | bytes 3145744 | tf_op jit(solution)/shard_map/all_gather | solution.py:269
  856.5 3.9 convolution_convert_fusion.9
  863.1 24.1 %all-gather.21.cloned.1.call-done = bf16[2048,768]{1,0:T(8,128)(2,1)} async-done(((bf16[512,768]{1,0:T(8,128)(2,1)}), bf16[2048,768]{1,0:T(8,128)(2,1)}) %all-gather.21.cloned.1.call-update) | async-done | bytes 3145744 | tf_op jit(solution)/shard_map/all_gather | solution.py:269
  887.3 3.9 convolution_convert_fusion.8
  899.4 40.0 %while.55 = (s32[]{:T(128)}, bf16[4,512,3,64]{1,3,2,0:T(8,128)(2,1)}, bf16[4,512,3,64]{1,3,2,0:T(8,128)(2,1)}, bf16[4,512,3,64]{1,3,2,0:T(8,128)(2,1)}, bf16[4,5...) while((s32[]{:T(128)}, ...), condition=%wide.region_51.53_spmd, body=%wide.region_49.52_spmd.sunk | while | flops 510884864 | bytes 25598088 | solution.py:277
  945.4 4.0 convolution_convert_fusion.4
  952.4 36.4 %while.54 = (s32[]{:T(128)}, bf16[4,512,3,64]{1,3,2,0:T(8,128)(2,1)}, bf16[4,512,3,64]{1,3,2,0:T(8,128)(2,1)}, bf16[4,512,3,64]{1,3,2,0:T(8,128)(2,1)}, bf16[4,5...) while((s32[]{:T(128)}, ...), condition=%wide.region_40.42_spmd, body=%wide.region_38.41_spmd.sunk | while | flops 510884864 | bytes 25598088 | solution.py:277
  993.9 4.0 convolution_convert_fusion.5
  998.2 5.7 fusion.211
  1007.5 4.2 convolution_add_fusion
  1011.7 4.2 convolution_add_fusion.1
  1035.6 22.8 %all-reduce.4 = (f32[576]{0:T(1024)S(1)}, f32[768]{0:T(1024)}) all-reduce(f32[576]{0:T(1024)S(1)} %add.358, f32[768]{0:T(1024)S(1)} %add.364), channel_id=1, replica_groups=mesh['dp'=8,'mp'=4] {'dp'}, use_global_device_ids=true, to_apply=%region_56.58 | all-reduce | flops 1344 | bytes 10752 | tf_op jit(solution)/shard_map/psum | solution.py:298
  1064.6 41.6 %all-reduce.2 = (f32[]{:T(128)}, f32[768]{0:T(1024)}, f32[768]{0:T(1024)}, f32[768]{0:T(1024)}, f32[768]{0:T(1024)}, /*index=5*/f32[768]{0:T(1024)}, f32[768]{0:T(1024)}) all-reduce(f32[]{:T(128)S(6)} %add.349, f32[768]{0:T(1024)S(1)} %add.360, f32[768]{0:T(1024)S(1)} %add.361, ...), channel_id=1, replica_groups=mesh['dp'=8,'mp'=4] {'dp','mp'}, use_global_device_ids=true, to_apply=%region_30.32 | all-reduce | flops 4609 | bytes 36872 | tf_op jit(solution)/shard_map/psum | solution.py:301
  1106.2 3.8 pad_maximum_fusion
  1110.0 168.0 %all-reduce.11.cloned.1.call-done = (f32[768,576]{0,1:T(8,128)}, f32[192,768]{1,0:T(8,128)}, f32[768,768]{1,0:T(8,128)}, f32[768,768]{1,0:T(8,128)}) async-done(((f32[768,576]{0,1:T(8,128)}, f32[192,768]{1,0:T(8,128)}, f32[768,768]{1,0:T(8,128)}, f32[768,768]{1,0:T(8,128)}), (f32[768,576]{0,1:T(8,128)}, f32[192,768]{1,0:T(8,128)}, f32[768,768]{1,0:T(8,128)}, ...) | async-done | bytes 7077904 | tf_op jit(solution)/shard_map/psum | solution.py:298
  (508 shorter events, 295.4 us)
Async XLA Ops:
  7.2 253.4 %copy-start = (bf16[768,768]{1,0:T(8,128)(2,1)S(1)}, bf16[768,768]{1,0:T(8,128)(2,1)}, u32[]{:S(2)}) copy-start(bf16[768,768]{1,0:T(8,128)(2,1)} %param.40) | copy-start | bytes 3538948
  7.2 22.3 %copy-start.98 = (bf16[192]{0:T(256)(128)(2,1)S(1)}, bf16[192]{0:T(256)(128)(2,1)}, u32[]{:S(2)}) copy-start(bf16[192]{0:T(256)(128)(2,1)} %param.35) | copy-start | bytes 1156
  7.2 22.3 %copy-start.99 = (bf16[192]{0:T(256)(128)(2,1)S(1)}, bf16[192]{0:T(256)(128)(2,1)}, u32[]{:S(2)}) copy-start(bf16[192]{0:T(256)(128)(2,1)} %param.32) | copy-start | bytes 1156
  7.2 25.3 %copy-start.93 = (s32[2,4]{1,0:T(2,128)S(1)}, s32[2,4]{1,0:T(2,128)}, u32[]{:S(2)}) copy-start(s32[2,4]{1,0:T(2,128)} %param.29) | copy-start | bytes 100
  7.2 178.1 %reduce-scatter.9.cloned.1.call-start = ((), (), s32[]{:S(2)}) async-start(), calls=%async_computation.8 | async-start | bytes 3932160 | tf_op jit(solution)/shard_map/reduce_scatter | solution.py:171
  9.7 17.8 %collective-permute-start = (bf16[512,768]{1,0:T(8,128)(2,1)S(1)}, bf16[512,768]{1,0:T(8,128)(2,1)S(1)}, u32[]{:S(2)}, u32[]{:S(2)}) collective-permute-start(bf16[512,768]{1,0:T(8,128)(2,1)S(1)} %get-tuple-element.431), channel_id=1, source_target_pairs={{0,1},{1,2},{2,3},{3,0},{4,5},{5,6},{6,7},{7,4},{8,9},{9,10},{10,1... | collective-permute-start | bytes 2359304 | tf_op jit(solution)/shard_map/ppermute | solution.py:22
  10.2 31.8 %collective-permute-start.3 = (bf16[512,768]{1,0:T(8,128)(2,1)}, bf16[512,768]{1,0:T(8,128)(2,1)}, u32[]{:S(2)}, u32[]{:S(2)}) collective-permute-start(bf16[512,768]{1,0:T(8,128)(2,1)} %get-tuple-element.430), channel_id=1, source_target_pairs={{0,1},{1,2},{2,3},{3,0},{4,5},{5,6},{6,7},{7,4},{8,9},{9,10},{10,1... | collective-permute-start | bytes 2359304 | tf_op jit(solution)/shard_map/ppermute | solution.py:22
  12.8 33.5 %collective-permute-start.2 = (bf16[512,768]{1,0:T(8,128)(2,1)S(1)}, bf16[512,768]{1,0:T(8,128)(2,1)S(1)}, u32[]{:S(2)}, u32[]{:S(2)}) collective-permute-start(bf16[512,768]{1,0:T(8,128)(2,1)S(1)} %get-tuple-element.431), channel_id=1, source_target_pairs={{0,3},{1,0},{2,1},{3,2},{4,7},{5,4},{6,5},{7,6},{8,11},{9,8},{10,9... | collective-permute-start | bytes 2359304 | tf_op jit(solution)/shard_map/ppermute | solution.py:24
  27.5 28.1 %collective-permute-start.1 = (bf16[512,768]{1,0:T(8,128)(2,1)S(1)}, bf16[512,768]{1,0:T(8,128)(2,1)}, u32[]{:S(2)}, u32[]{:S(2)}) collective-permute-start(bf16[512,768]{1,0:T(8,128)(2,1)S(1)} %collective-permute-done), channel_id=1, source_target_pairs={{0,1},{1,2},{2,3},{3,0},{4,5},{5,6},{6,7},{7,4},{8,9},{9,10},{10,1... | collective-permute-start | bytes 2359304 | tf_op jit(solution)/shard_map/ppermute | solution.py:22
  29.5 87.6 %collective-permute-start.5 = (bf16[512,768]{1,0:T(8,128)(2,1)}, bf16[512,768]{1,0:T(8,128)(2,1)}, u32[]{:S(2)}, u32[]{:S(2)}) collective-permute-start(bf16[512,768]{1,0:T(8,128)(2,1)} %get-tuple-element.430), channel_id=1, source_target_pairs={{0,3},{1,0},{2,1},{3,2},{4,7},{5,4},{6,5},{7,6},{8,11},{9,8},{10,9... | collective-permute-start | bytes 2359304 | tf_op jit(solution)/shard_map/ppermute | solution.py:24
  32.6 48.8 %copy-start.50 = (bf16[768,576]{0,1:T(8,128)(2,1)}, bf16[768,576]{0,1:T(8,128)(2,1)S(1)}, u32[]{:S(2)}) copy-start(bf16[768,576]{0,1:T(8,128)(2,1)S(1)} %constant_dynamic-update-slice_fusion) | copy-start | bytes 2654212
  42.0 75.1 %collective-permute-start.4 = (bf16[512,768]{1,0:T(8,128)(2,1)}, bf16[512,768]{1,0:T(8,128)(2,1)}, u32[]{:S(2)}, u32[]{:S(2)}) collective-permute-start(bf16[512,768]{1,0:T(8,128)(2,1)} %collective-permute-done.3), channel_id=1, source_target_pairs={{0,1},{1,2},{2,3},{3,0},{4,5},{5,6},{6,7},{7,4},{8,9},{9,10},{10,1... | collective-permute-start | bytes 2359304 | tf_op jit(solution)/shard_map/ppermute | solution.py:22
  114.5 12.5 copy-start.12
  114.5 12.5 copy-start.14
  114.5 12.5 copy-start.94
  117.1 25.3 %copy-start.25 = (bf16[24,8,4,512]{3,1,2,0:T(8,128)(2,1)}, bf16[24,8,4,512]{3,1,2,0:T(8,128)(2,1)S(1)}, u32[]{:S(2)}) copy-start(bf16[24,8,4,512]{3,1,2,0:T(8,128)(2,1)S(1)} %copy.108) | copy-start | bytes 2359300
  117.1 11.7 copy-start.51
  145.2 80.8 %reduce-scatter.13.cloned.1.call-start = ((), (), s32[]{:S(2)}) async-start(), calls=%async_computation.11 | async-start | bytes 3932160 | tf_op jit(solution)/shard_map/reduce_scatter | solution.py:171
  171.4 13.9 %copy-start.1 = (bf16[2,512,768]{2,1,0:T(8,128)(2,1)S(1)}, bf16[2,512,768]{2,1,0:T(8,128)(2,1)}, u32[]{:S(2)}) copy-start(bf16[2,512,768]{2,1,0:T(8,128)(2,1)} %param.28) | copy-start | bytes 4718596
  171.5 89.1 %all-gather.13.cloned.1.call-start = ((), (), s32[]{:S(2)}) async-start(), calls=%async_computation.12 | async-start | bytes 3932160 | tf_op jit(solution)/shard_map/all_gather | solution.py:180
  185.3 44.5 %copy-start.6 = (bf16[512,768]{1,0:T(8,128)(2,1)S(1)}, bf16[512,768]{1,0:T(8,128)(2,1)}, u32[]{:S(2)}) copy-start(bf16[512,768]{1,0:T(8,128)(2,1)} %reduce-scatter.9.cloned.1.call-done) | copy-start | bytes 2359300
  186.9 221.8 %copy-start.56 = (f32[512]{0:T(512)}, f32[512]{0:T(512)S(1)}, u32[]{:S(2)}) copy-start(f32[512]{0:T(512)S(1)} %broadcast_multiply_fusion.7) | copy-start | bytes 6148
  228.2 180.5 %copy-start.54 = (f32[512]{0:T(512)}, f32[512]{0:T(512)S(1)}, u32[]{:S(2)}) copy-start(f32[512]{0:T(512)S(1)} %broadcast_multiply_fusion.5) | copy-start | bytes 6148
  231.9 59.3 %all-gather.11.cloned.1.call-start = ((), (), s32[]{:S(2)}) async-start(), calls=%async_computation.9 | async-start | bytes 3932160 | tf_op jit(solution)/shard_map/all_gather | solution.py:180
  232.4 135.6 %reduce-scatter.11.cloned.1.call-start = ((), (), s32[]{:S(2)}) async-start(), calls=%async_computation.10 | async-start | bytes 3932160 | tf_op jit(solution)/shard_map/reduce_scatter | solution.py:185
  291.1 34.9 %copy-start.101 = (bf16[768,768]{1,0:T(8,128)(2,1)S(1)}, bf16[768,768]{1,0:T(8,128)(2,1)}, u32[]{:S(2)}) copy-start(bf16[768,768]{1,0:T(8,128)(2,1)} %param.42) | copy-start | bytes 3538948
  330.0 78.6 %reduce-scatter.15.cloned.1.call-start = ((), (), s32[]{:S(2)}) async-start(), calls=%async_computation.13 | async-start | bytes 3932160 | tf_op jit(solution)/shard_map/reduce_scatter | solution.py:185
  336.6 302.9 %all-reduce.9.cloned.1.call-start = ((), (), s32[]{:S(2)}) async-start(), calls=%async_computation.22 | async-start | bytes 393216
  518.6 165.1 %all-gather.15.cloned.1.call-start = ((), (), s32[]{:S(2)}) async-start(), calls=%async_computation.14 | async-start | bytes 3932160 | tf_op jit(solution)/shard_map/all_gather | solution.py:241
  639.6 9.5 copy-start.61
  639.6 9.5 copy-start.63
  639.6 9.5 copy-start.69
  654.1 59.8 %all-gather.19.cloned.1.call-start = ((), (), s32[]{:S(2)}) async-start(), calls=%async_computation.18 | async-start | bytes 3932160 | tf_op jit(solution)/shard_map/all_gather | solution.py:241
  654.8 36.5 %copy-start.73 = (f32[512]{0:T(512)}, f32[512]{0:T(512)S(1)}, u32[]{:S(2)}) copy-start(f32[512]{0:T(512)S(1)} %negate_multiply_fusion.3) | copy-start | bytes 6148
  657.3 117.0 %reduce-scatter.17.cloned.1.call-start = ((), (), s32[]{:S(2)}) async-start(), calls=%async_computation.15 | async-start | bytes 3932160 | tf_op jit(solution)/shard_map/reduce_scatter | solution.py:253
  657.4 56.5 %copy-start.89 = (f32[768]{0:T(1024)S(1)}, f32[768]{0:T(1024)}, u32[]{:S(2)}) copy-start(f32[768]{0:T(1024)} %convert_element_type.263) | copy-start | bytes 9220
  736.3 78.7 %reduce-scatter.21.cloned.1.call-start = ((), (), s32[]{:S(2)}) async-start(), calls=%async_computation.19 | async-start | bytes 3932160 | tf_op jit(solution)/shard_map/reduce_scatter | solution.py:253
  742.5 72.5 %copy-start.55 = (f32[512]{0:T(512)S(1)}, f32[512]{0:T(512)}, u32[]{:S(2)}) copy-start(f32[512]{0:T(512)} %copy-done.54) | copy-start | bytes 6148
  742.5 72.5 %copy-start.57 = (f32[512]{0:T(512)S(1)}, f32[512]{0:T(512)}, u32[]{:S(2)}) copy-start(f32[512]{0:T(512)} %copy-done.56) | copy-start | bytes 6148
  742.6 114.0 %all-gather.17.cloned.1.call-start = ((), (), s32[]{:S(2)}) async-start(), calls=%async_computation.16 | async-start | bytes 3932160 | tf_op jit(solution)/shard_map/all_gather | solution.py:269
  826.8 29.8 %copy-start.47 = (bf16[192,768]{1,0:T(8,128)(2,1)S(1)}, bf16[192,768]{1,0:T(8,128)(2,1)}, u32[]{:S(2)}) copy-start(bf16[192,768]{1,0:T(8,128)(2,1)} %param.36) | copy-start | bytes 884740
  827.8 59.4 %all-gather.21.cloned.1.call-start = ((), (), s32[]{:S(2)}) async-start(), calls=%async_computation.20 | async-start | bytes 3932160 | tf_op jit(solution)/shard_map/all_gather | solution.py:269
  829.5 228.9 %reduce-scatter.23.cloned.1.call-start = ((), (), s32[]{:S(2)}) async-start(), calls=%async_computation.21 | async-start | bytes 3932160 | tf_op jit(solution)/shard_map/reduce_scatter | solution.py:288
  860.5 26.8 %copy-start.48 = (bf16[192,768]{1,0:T(8,128)(2,1)S(1)}, bf16[192,768]{1,0:T(8,128)(2,1)}, u32[]{:S(2)}) copy-start(bf16[192,768]{1,0:T(8,128)(2,1)} %param.36) | copy-start | bytes 884740
  949.5 112.0 %reduce-scatter.19.cloned.1.call-start = ((), (), s32[]{:S(2)}) async-start(), calls=%async_computation.17 | async-start | bytes 3932160 | tf_op jit(solution)/shard_map/reduce_scatter | solution.py:288
  997.9 280.0 %all-reduce.11.cloned.1.call-start = ((), (), s32[]{:S(2)}) async-start(), calls=%async_computation.23 | async-start | bytes 14155776 | tf_op jit(solution)/shard_map/psum | solution.py:298
  1028.8 32.7 %copy-start.21 = (f32[512,768]{1,0:T(8,128)S(1)}, f32[512,768]{1,0:T(8,128)}, u32[]{:S(2)}) copy-start(f32[512,768]{1,0:T(8,128)} %copy-done.20) | copy-start | bytes 4718596
  1031.3 30.2 %copy-start.82 = (f32[512]{0:T(512)S(1)}, f32[512]{0:T(512)}, u32[]{:S(2)}) copy-start(f32[512]{0:T(512)} %copy-done.81) | copy-start | bytes 6148
  (79 other events, 280.1 us)
Sparse Core Ops, SparseCore 0:
  145.3 39.9 reduce-scatter.8
  188.0 37.9 reduce-scatter.12
  232.0 28.5 all-gather.12
  262.6 28.5 all-gather.10
  330.1 37.9 reduce-scatter.10
  370.6 37.9 reduce-scatter.14
  518.7 120.8 all-reduce.8
  654.2 29.4 all-gather.14
  685.3 28.5 all-gather.18
  736.4 37.9 reduce-scatter.16
  777.0 37.9 reduce-scatter.20
  828.0 28.5 all-gather.16
  858.7 28.5 all-gather.20
  949.6 37.9 reduce-scatter.22
  998.0 37.9 reduce-scatter.18
  1040.9 236.9 all-reduce.10
